TPU v7x, 512 devices: a whole 4x4x16 slice. The times are simulated.
512 devices in a mesh: dp: 8 (over y, x_lo), ctx: 64 (over z, x_hi, core).
Axes of the slice: x: 4 (x_hi: 2, x_lo: 2; x = x_hi * 2 + x_lo), y: 4, z: 16, core: 2. Of those that a mesh axis runs over, the one named last changes fastest.
Arguments:
- events: bfloat16 [8, 16384, 1024], P('dp', 'ctx'), may hold values from -6 to 6
- w_query: bfloat16 [1024, 512], replicated, may hold values from -0.1875 to 0.1875
- w_key: bfloat16 [1024, 512], replicated, may hold values from -0.1875 to 0.1875
- values: bfloat16 [8, 16384, 512], P('dp', 'ctx'), may hold values from -6 to 6
- grad_out: bfloat16 [8, 16384, 512], P('dp', 'ctx'), may hold values from -6 to 6
- lengths: int32 [8, 32], P('dp'), may hold values from 1 to 768, 16384 in all within a row
- stream_shift: int32 [8], P('dp'), may hold values from 0 to 16383
- block_keep: int32 [8, 128], P('dp'), may hold values 0 or 1
Outputs:
- attended: bfloat16 [8, 16384, 512], P('dp', 'ctx')
- grad_values: bfloat16 [8, 16384, 512], P('dp', 'ctx')
- grad_wq: bfloat16 [1024, 512], P('ctx')
- grad_wk: bfloat16 [1024, 512], P('ctx')
Inputs may be any that keep to these rules, and one draw needn't show every extreme that they name: The lengths of a stream sum to 16384; the longest is exactly 768.
All inputs are finite; a program needn't handle non-finite values. No bound on the sum of `block_keep` on one device may be relied on, other than what follows from the above.
Results may differ from a plain program's by a relative error of at most 0.011.
Values may be sent and summed in bfloat16 or wider, within the bound.
A program may use at most 64 MiB of HBM per device.

v0:
```python
import jax
import jax.numpy as jnp
from jax import lax
from jax.sharding import PartitionSpec as P

HD = 128
SPAN = 3
BLOCK = 128
MAXLEN = 768


def from_behind(value, axis, steps):
    count = lax.axis_size(axis)
    pairs = [(source, (source + steps) % count) for source in range(count)]
    return lax.ppermute(value, axis, pairs)


def tile_terms(query, grad, key, value, valid, scale, alpha):
    z = jnp.einsum("qhd,khd->hqk", query, key, preferred_element_type=jnp.float32) * alpha
    sig = jax.nn.sigmoid(z)
    weight = valid[None, :, :].astype(jnp.float32) * scale
    att = (z * sig * weight).astype(jnp.bfloat16)
    out = jnp.einsum("hqk,khd->qhd", att, value, preferred_element_type=jnp.float32)
    dprod = jnp.einsum("qhd,khd->hqk", grad, value, preferred_element_type=jnp.float32)
    dsc = (dprod * sig * (1.0 + z * (1.0 - sig)) * weight * alpha).astype(jnp.bfloat16)
    dquery = jnp.einsum("hqk,khd->qhd", dsc, key, preferred_element_type=jnp.float32)
    dkey = jnp.einsum("hqk,qhd->khd", dsc, query, preferred_element_type=jnp.float32)
    dvalue = jnp.einsum("hqk,qhd->khd", att, grad, preferred_element_type=jnp.float32)
    return (out, dquery, dkey, dvalue)


def body(events, w_query, w_key, values, grad_out, lengths, stream_shift, block_keep):
    rows = events.shape[1]
    features = w_query.shape[1]
    nheads = features // HD
    alpha = 1.0 / HD**0.5
    scale = 1.0 / MAXLEN**0.5
    local = events[0]
    queries = jnp.dot(local, w_query, preferred_element_type=jnp.float32).astype(jnp.bfloat16)
    keys = jnp.dot(local, w_key, preferred_element_type=jnp.float32).astype(jnp.bfloat16)
    queries = queries.reshape(rows, nheads, HD)
    keys = keys.reshape(rows, nheads, HD)
    vals = values[0].reshape(rows, nheads, HD)
    cotan = grad_out[0].reshape(rows, nheads, HD)
    cycle_size = lax.axis_size("ctx")
    myself = lax.axis_index("ctx")
    total = rows * cycle_size
    ends = jnp.cumsum(lengths[0])
    offset = stream_shift[0]
    keep = block_keep[0]
    blocks_all = jnp.arange(keep.shape[0], dtype=jnp.int32)
    within = jnp.arange(rows, dtype=jnp.int32)

    def describe(anchor):
        anchor = jnp.remainder(anchor, cycle_size)
        position = jnp.remainder(anchor * rows + within - offset, total)
        owner = jnp.sum((position[:, None] >= ends[None, :]).astype(jnp.int32), axis=1)
        which = position // BLOCK
        kept = (
            jnp.sum(jnp.where(which[:, None] == blocks_all[None, :], keep[None, :], 0), axis=1) > 0
        )
        return (position, owner, kept)

    zeros = jnp.zeros((rows, nheads, HD), jnp.float32)
    qinfo = describe(myself)
    moving = (keys, vals)
    carried = (zeros, zeros)
    out_acc = zeros
    dq_acc = zeros
    for step in range(SPAN + 1):
        if step > 0:
            moving = from_behind((moving[0], moving[1]), "ctx", 1)
            carried = (
                from_behind(carried[0].astype(jnp.bfloat16), "ctx", 1).astype(jnp.float32),
                from_behind(carried[1].astype(jnp.bfloat16), "ctx", 1).astype(jnp.float32),
            )
        kinfo = describe(myself - step)
        o, a, b, c = tile_terms(
            queries,
            cotan,
            moving[0],
            moving[1],
            (qinfo[1][:, None] == kinfo[1][None, :])
            & (kinfo[0][None, :] <= qinfo[0][:, None])
            & kinfo[2][None, :],
            scale,
            alpha,
        )
        out_acc = out_acc + o
        dq_acc = dq_acc + a
        carried = (carried[0] + b, carried[1] + c)
    carried = (
        from_behind(carried[0].astype(jnp.bfloat16), "ctx", -SPAN).astype(jnp.float32),
        from_behind(carried[1].astype(jnp.bfloat16), "ctx", -SPAN).astype(jnp.float32),
    )
    dk_acc, dv_acc = carried
    attended = out_acc.reshape(1, rows, features).astype(jnp.bfloat16)
    grad_values = dv_acc.reshape(1, rows, features).astype(jnp.bfloat16)
    dq_b = dq_acc.reshape(rows, features).astype(jnp.bfloat16)
    dk_b = dk_acc.reshape(rows, features).astype(jnp.bfloat16)
    joined = jnp.concatenate([dq_b, dk_b], axis=1)
    width_rows = local.shape[1]
    share = width_rows // cycle_size
    terms = jnp.einsum("rd,rf->df", local, joined, preferred_element_type=jnp.float32)
    summed = lax.psum(terms, ("dp", "ctx"))
    mine = lax.dynamic_slice_in_dim(summed, myself * share, share, 0)
    grad_wq = mine[:, :features].astype(jnp.bfloat16)
    grad_wk = mine[:, features:].astype(jnp.bfloat16)
    return (attended, grad_values, grad_wq, grad_wk)


def solution(mesh):
    placed = (
        P("dp", "ctx", None),
        P(),
        P(),
        P("dp", "ctx", None),
        P("dp", "ctx", None),
        P("dp", None),
        P("dp"),
        P("dp", None),
    )
    return jax.shard_map(
        body,
        mesh=mesh,
        in_specs=placed,
        out_specs=(P("dp", "ctx", None), P("dp", "ctx", None), P("ctx", None), P("ctx", None)),
        check_vma=False,
    )
```

profile of v0, /device:TPU:7, one launch (start us, length us, event | category | flops | bytes accessed | tf_op | source)
XLA Modules:
  0.0 291.1 jit_solution(15227647348382941098)
XLA Ops:
  0.6 1.2 copy.87
  1.8 4.9 %collective-permute-start.1 = (bf16[256,4,128]{0,2,1:T(8,128)(2,1)S(1)}, bf16[256,4,128]{0,2,1:T(8,128)(2,1)S(1)}, u32[]{:S(2)}, u32[]{:S(2)}) collective-permute-start(bf16[256,4,128]{0,2,1:T(8,128)(2,1)S(1)} %bitcast.101), channel_id=1, source_target_pairs={{0,1},{1,2},{2,3},{3,4},{4,5},{5,6},{6,7},{7,8},{8,9},{9,10},{10,1... | collective-permute-start | bytes 786440 | tf_op jit(solution)/shard_map/ppermute | solution.py:15
  6.8 1.5 fusion.20
  8.3 0.7 copy.157
  9.0 1.9 collective-permute-start
  11.7 1.0 select_reduce_fusion
  12.8 0.7 copy.86
  13.7 1.0 reshape_squeeze.7
  14.8 1.8 convolution_convert_fusion.3
  16.8 1.2 and_select_fusion
  18.0 0.5 multiply_convert_fusion.3
  18.6 0.5 fusion.15
  19.1 1.0 fusion.19
  20.1 4.1 %collective-permute-start.10 = (bf16[256,4,128]{0,2,1:T(8,128)(2,1)}, bf16[256,4,128]{0,2,1:T(8,128)(2,1)}, u32[]{:S(2)}, u32[]{:S(2)}) collective-permute-start(bf16[256,4,128]{0,2,1:T(8,128)(2,1)} %fusion.19), channel_id=1, source_target_pairs={{0,1},{1,2},{2,3},{3,4},{4,5},{5,6},{6,7},{7,8},{8,9},{9,10},{10,1... | collective-permute-start | bytes 786440 | tf_op jit(solution)/shard_map/ppermute | solution.py:15
  24.2 1.1 fusion.18
  25.3 1.9 collective-permute-start.6
  27.8 1.6 multiply_convert_fusion.2
  30.0 1.2 add_convert_fusion.2
  31.2 4.8 %collective-permute-start.11 = (bf16[256,4,128]{0,2,1:T(8,128)(2,1)S(1)}, bf16[256,4,128]{0,2,1:T(8,128)(2,1)S(1)}, u32[]{:S(2)}, u32[]{:S(2)}) collective-permute-start(bf16[256,4,128]{0,2,1:T(8,128)(2,1)S(1)} %add_convert_fusion.2), channel_id=1, source_target_pairs={{0,1},{1,2},{2,3},{3,4},{4,5},{5,6},{6,7},{7,8},{8,9},{9,10},{10,1... | collective-permute-start | bytes 786440 | tf_op jit(solution)/shard_map/ppermute | solution.py:15
  36.0 1.3 add_convert_fusion.5
  37.3 1.9 collective-permute-start.7
  39.2 4.1 %collective-permute-start.3 = (bf16[256,4,128]{0,2,1:T(8,128)(2,1)S(1)}, bf16[256,4,128]{0,2,1:T(8,128)(2,1)S(1)}, u32[]{:S(2)}, u32[]{:S(2)}) collective-permute-start(bf16[256,4,128]{0,2,1:T(8,128)(2,1)S(1)} %collective-permute-done.1), channel_id=1, source_target_pairs={{0,1},{1,2},{2,3},{3,4},{4,5},{5,6},{6,7},{7,8},{8,9},{9,10},{10,1... | collective-permute-start | bytes 786440 | tf_op jit(solution)/shard_map/ppermute | solution.py:15
  43.4 1.9 collective-permute-start.2
  45.6 1.3 convolution_add_fusion.2
  46.9 2.7 collective-permute-done.2
  49.6 0.5 multiply_convert_fusion.1
  50.2 0.5 fusion.13
  51.0 6.7 %collective-permute-start.12 = (bf16[256,4,128]{0,2,1:T(8,128)(2,1)S(1)}, bf16[256,4,128]{0,2,1:T(8,128)(2,1)S(1)}, u32[]{:S(2)}, u32[]{:S(2)}) collective-permute-start(bf16[256,4,128]{0,2,1:T(8,128)(2,1)S(1)} %add_convert_fusion.1), channel_id=1, source_target_pairs={{0,1},{1,2},{2,3},{3,4},{4,5},{5,6},{6,7},{7,8},{8,9},{9,10},{10,1... | collective-permute-start | bytes 786440 | tf_op jit(solution)/shard_map/ppermute | solution.py:15
  58.1 0.7 add_convert_fusion.4
  58.8 1.9 collective-permute-start.8
  60.7 3.9 %collective-permute-start.5 = (bf16[256,4,128]{0,2,1:T(8,128)(2,1)S(1)}, bf16[256,4,128]{0,2,1:T(8,128)(2,1)S(1)}, u32[]{:S(2)}, u32[]{:S(2)}) collective-permute-start(bf16[256,4,128]{0,2,1:T(8,128)(2,1)S(1)} %collective-permute-done.3), channel_id=1, source_target_pairs={{0,1},{1,2},{2,3},{3,4},{4,5},{5,6},{6,7},{7,8},{8,9},{9,10},{10,1... | collective-permute-start | bytes 786440 | tf_op jit(solution)/shard_map/ppermute | solution.py:15
  64.6 1.9 collective-permute-start.4
  67.2 3.5 %collective-permute-done.4 = bf16[256,4,128]{2,0,1:T(8,128)(2,1)S(1)} collective-permute-done((bf16[256,4,128]{2,0,1:T(8,128)(2,1)S(1)}, bf16[256,4,128]{2,0,1:T(8,128)(2,1)S(1)}, u32[]{:S(2)}, u32[]{:S(2)}) %collective-permute-start.4) | collective-permute-done | bytes 262176 | tf_op jit(solution)/shard_map/ppermute | solution.py:15
  70.7 0.5 multiply_convert_fusion
  71.4 0.5 fusion.12
  72.2 1.0 fusion.16
  73.2 0.8 add_convert_fusion
  74.0 1.8 copy.117
  75.8 9.6 %collective-permute-start.13 = (bf16[256,4,128]{0,2,1:T(8,128)(2,1)}, bf16[256,4,128]{0,2,1:T(8,128)(2,1)}, u32[]{:S(2)}, u32[]{:S(2)}) collective-permute-start(bf16[256,4,128]{0,2,1:T(8,128)(2,1)} %add_convert_fusion), channel_id=1, source_target_pairs={{0,61},{1,62},{2,63},{3,0},{4,1},{5,2},{6,3},{7,4},{8,5},{9,6},{10... | collective-permute-start | bytes 786440 | tf_op jit(solution)/shard_map/ppermute | solution.py:15
  85.8 1.0 add_convert_fusion.3
  86.8 2.1 collective-permute-start.9
  88.9 1.3 fusion.17
  90.2 4.3 %collective-permute-done.9 = bf16[256,4,128]{2,0,1:T(8,128)(2,1)S(1)} collective-permute-done((bf16[256,4,128]{2,0,1:T(8,128)(2,1)S(1)}, bf16[256,4,128]{2,0,1:T(8,128)(2,1)S(1)}, u32[]{:S(2)}, u32[]{:S(2)}) %collective-permute-start.9) | collective-permute-done | bytes 262176 | tf_op jit(solution)/shard_map/ppermute | solution.py:15
  94.6 0.8 copy.118
  95.5 3.6 %convolution_bitcast_fusion = f32[1024,1024]{0,1:T(8,128)} fusion(bf16[256,512]{0,1:T(8,128)(2,1)} %bitcast.18, bf16[256,512]{0,1:T(8,128)(2,1)S(1)} %bitcast.104, bf16[1,256,1024]{2,1,0:T(8,128)(2,1)S(1)} %copy-done.1), kind=kOutput, calls=%fused_computation | convolution fusion | flops 537919488 | bytes 5242880 | tf_op jit(solution)/shard_map/rd,rf->df/dot_general | solution.py:104
  99.1 190.5 %all-reduce.1 = bf16[1024,1024]{0,1:T(8,128)(2,1)S(1)} all-reduce(f32[1024,1024]{0,1:T(8,128)} %convolution_bitcast_fusion), channel_id=1, replica_groups=mesh['dp'=8,'ctx'=64] {'dp','ctx'}, use_global_device_ids=true, to_apply=%region_9.10 | all-reduce | flops 1048576 | bytes 6291456 | tf_op jit(solution)/shard_map/psum | solution.py:105
  289.8 0.7 copy.120
  290.5 0.7 copy.119
  (49 shorter events, 4.3 us)
Async XLA Ops:
  0.6 6.2 %copy-start = (bf16[1024,512]{1,0:T(8,128)(2,1)S(1)}, bf16[1024,512]{1,0:T(8,128)(2,1)}, u32[]{:S(2)}) copy-start(bf16[1024,512]{1,0:T(8,128)(2,1)} %param.10) | copy-start | bytes 3145732
  1.8 27.6 %collective-permute-start.1 = (bf16[256,4,128]{0,2,1:T(8,128)(2,1)S(1)}, bf16[256,4,128]{0,2,1:T(8,128)(2,1)S(1)}, u32[]{:S(2)}, u32[]{:S(2)}) collective-permute-start(bf16[256,4,128]{0,2,1:T(8,128)(2,1)S(1)} %bitcast.101), channel_id=1, source_target_pairs={{0,1},{1,2},{2,3},{3,4},{4,5},{5,6},{6,7},{7,8},{8,9},{9,10},{10,1... | collective-permute-start | bytes 786440 | tf_op jit(solution)/shard_map/ppermute | solution.py:15
  9.0 18.8 %collective-permute-start = (bf16[256,4,128]{2,0,1:T(8,128)(2,1)}, bf16[256,4,128]{2,0,1:T(8,128)(2,1)}, u32[]{:S(2)}, u32[]{:S(2)}) collective-permute-start(bf16[256,4,128]{2,0,1:T(8,128)(2,1)} %bitcast.88), channel_id=1, source_target_pairs={{0,1},{1,2},{2,3},{3,4},{4,5},{5,6},{6,7},{7,8},{8,9},{9,10},{10,1... | collective-permute-start | bytes 786440 | tf_op jit(solution)/shard_map/ppermute | solution.py:15
  20.1 9.9 %collective-permute-start.10 = (bf16[256,4,128]{0,2,1:T(8,128)(2,1)}, bf16[256,4,128]{0,2,1:T(8,128)(2,1)}, u32[]{:S(2)}, u32[]{:S(2)}) collective-permute-start(bf16[256,4,128]{0,2,1:T(8,128)(2,1)} %fusion.19), channel_id=1, source_target_pairs={{0,1},{1,2},{2,3},{3,4},{4,5},{5,6},{6,7},{7,8},{8,9},{9,10},{10,1... | collective-permute-start | bytes 786440 | tf_op jit(solution)/shard_map/ppermute | solution.py:15
  25.3 10.7 %collective-permute-start.6 = (bf16[256,4,128]{2,0,1:T(8,128)(2,1)}, bf16[256,4,128]{2,0,1:T(8,128)(2,1)}, u32[]{:S(2)}, u32[]{:S(2)}) collective-permute-start(bf16[256,4,128]{2,0,1:T(8,128)(2,1)} %fusion.18), channel_id=1, source_target_pairs={{0,1},{1,2},{2,3},{3,4},{4,5},{5,6},{6,7},{7,8},{8,9},{9,10},{10,1... | collective-permute-start | bytes 786440 | tf_op jit(solution)/shard_map/ppermute | solution.py:15
  27.5 1.9 copy-start.4
  30.0 19.6 %copy-start.3 = (f32[256,256]{1,0:T(8,128)S(1)}, f32[256,256]{1,0:T(8,128)}, u32[]{:S(2)}) copy-start(f32[256,256]{1,0:T(8,128)} %get-tuple-element.27) | copy-start | bytes 786436
  31.2 19.7 %collective-permute-start.11 = (bf16[256,4,128]{0,2,1:T(8,128)(2,1)S(1)}, bf16[256,4,128]{0,2,1:T(8,128)(2,1)S(1)}, u32[]{:S(2)}, u32[]{:S(2)}) collective-permute-start(bf16[256,4,128]{0,2,1:T(8,128)(2,1)S(1)} %add_convert_fusion.2), channel_id=1, source_target_pairs={{0,1},{1,2},{2,3},{3,4},{4,5},{5,6},{6,7},{7,8},{8,9},{9,10},{10,1... | collective-permute-start | bytes 786440 | tf_op jit(solution)/shard_map/ppermute | solution.py:15
  37.3 20.8 %collective-permute-start.7 = (bf16[256,4,128]{2,0,1:T(8,128)(2,1)S(1)}, bf16[256,4,128]{2,0,1:T(8,128)(2,1)S(1)}, u32[]{:S(2)}, u32[]{:S(2)}) collective-permute-start(bf16[256,4,128]{2,0,1:T(8,128)(2,1)S(1)} %add_convert_fusion.5), channel_id=1, source_target_pairs={{0,1},{1,2},{2,3},{3,4},{4,5},{5,6},{6,7},{7,8},{8,9},{9,10},{10,1... | collective-permute-start | bytes 786440 | tf_op jit(solution)/shard_map/ppermute | solution.py:15
  39.2 10.9 %collective-permute-start.3 = (bf16[256,4,128]{0,2,1:T(8,128)(2,1)S(1)}, bf16[256,4,128]{0,2,1:T(8,128)(2,1)S(1)}, u32[]{:S(2)}, u32[]{:S(2)}) collective-permute-start(bf16[256,4,128]{0,2,1:T(8,128)(2,1)S(1)} %collective-permute-done.1), channel_id=1, source_target_pairs={{0,1},{1,2},{2,3},{3,4},{4,5},{5,6},{6,7},{7,8},{8,9},{9,10},{10,1... | collective-permute-start | bytes 786440 | tf_op jit(solution)/shard_map/ppermute | solution.py:15
  43.4 6.2 %collective-permute-start.2 = (bf16[256,4,128]{2,0,1:T(8,128)(2,1)}, bf16[256,4,128]{2,0,1:T(8,128)(2,1)S(1)}, u32[]{:S(2)}, u32[]{:S(2)}) collective-permute-start(bf16[256,4,128]{2,0,1:T(8,128)(2,1)} %collective-permute-done), channel_id=1, source_target_pairs={{0,1},{1,2},{2,3},{3,4},{4,5},{5,6},{6,7},{7,8},{8,9},{9,10},{10,1... | collective-permute-start | bytes 786440 | tf_op jit(solution)/shard_map/ppermute | solution.py:15
  50.7 20.0 %copy-start.2 = (f32[256,256]{1,0:T(8,128)S(1)}, f32[256,256]{1,0:T(8,128)}, u32[]{:S(2)}) copy-start(f32[256,256]{1,0:T(8,128)} %get-tuple-element.26) | copy-start | bytes 786436
  51.0 22.2 %collective-permute-start.12 = (bf16[256,4,128]{0,2,1:T(8,128)(2,1)S(1)}, bf16[256,4,128]{0,2,1:T(8,128)(2,1)S(1)}, u32[]{:S(2)}, u32[]{:S(2)}) collective-permute-start(bf16[256,4,128]{0,2,1:T(8,128)(2,1)S(1)} %add_convert_fusion.1), channel_id=1, source_target_pairs={{0,1},{1,2},{2,3},{3,4},{4,5},{5,6},{6,7},{7,8},{8,9},{9,10},{10,1... | collective-permute-start | bytes 786440 | tf_op jit(solution)/shard_map/ppermute | solution.py:15
  58.8 26.9 %collective-permute-start.8 = (bf16[256,4,128]{2,0,1:T(8,128)(2,1)}, bf16[256,4,128]{2,0,1:T(8,128)(2,1)}, u32[]{:S(2)}, u32[]{:S(2)}) collective-permute-start(bf16[256,4,128]{2,0,1:T(8,128)(2,1)} %add_convert_fusion.4), channel_id=1, source_target_pairs={{0,1},{1,2},{2,3},{3,4},{4,5},{5,6},{6,7},{7,8},{8,9},{9,10},{10,1... | collective-permute-start | bytes 786440 | tf_op jit(solution)/shard_map/ppermute | solution.py:15
  60.7 10.5 %collective-permute-start.5 = (bf16[256,4,128]{0,2,1:T(8,128)(2,1)S(1)}, bf16[256,4,128]{0,2,1:T(8,128)(2,1)S(1)}, u32[]{:S(2)}, u32[]{:S(2)}) collective-permute-start(bf16[256,4,128]{0,2,1:T(8,128)(2,1)S(1)} %collective-permute-done.3), channel_id=1, source_target_pairs={{0,1},{1,2},{2,3},{3,4},{4,5},{5,6},{6,7},{7,8},{8,9},{9,10},{10,1... | collective-permute-start | bytes 786440 | tf_op jit(solution)/shard_map/ppermute | solution.py:15
  64.6 6.1 %collective-permute-start.4 = (bf16[256,4,128]{2,0,1:T(8,128)(2,1)S(1)}, bf16[256,4,128]{2,0,1:T(8,128)(2,1)S(1)}, u32[]{:S(2)}, u32[]{:S(2)}) collective-permute-start(bf16[256,4,128]{2,0,1:T(8,128)(2,1)S(1)} %collective-permute-done.2), channel_id=1, source_target_pairs={{0,1},{1,2},{2,3},{3,4},{4,5},{5,6},{6,7},{7,8},{8,9},{9,10},{10,1... | collective-permute-start | bytes 786440 | tf_op jit(solution)/shard_map/ppermute | solution.py:15
  70.7 0.7 copy-start.5
  72.2 23.3 %copy-start.1 = (bf16[1,256,1024]{2,1,0:T(8,128)(2,1)S(1)}, bf16[1,256,1024]{2,1,0:T(8,128)(2,1)}, u32[]{:S(2)}) copy-start(bf16[1,256,1024]{2,1,0:T(8,128)(2,1)} %param.8) | copy-start | bytes 1572868
  75.8 19.7 %collective-permute-start.13 = (bf16[256,4,128]{0,2,1:T(8,128)(2,1)}, bf16[256,4,128]{0,2,1:T(8,128)(2,1)}, u32[]{:S(2)}, u32[]{:S(2)}) collective-permute-start(bf16[256,4,128]{0,2,1:T(8,128)(2,1)} %add_convert_fusion), channel_id=1, source_target_pairs={{0,61},{1,62},{2,63},{3,0},{4,1},{5,2},{6,3},{7,4},{8,5},{9,6},{10... | collective-permute-start | bytes 786440 | tf_op jit(solution)/shard_map/ppermute | solution.py:15
  86.8 7.7 %collective-permute-start.9 = (bf16[256,4,128]{2,0,1:T(8,128)(2,1)S(1)}, bf16[256,4,128]{2,0,1:T(8,128)(2,1)S(1)}, u32[]{:S(2)}, u32[]{:S(2)}) collective-permute-start(bf16[256,4,128]{2,0,1:T(8,128)(2,1)S(1)} %add_convert_fusion.3), channel_id=1, source_target_pairs={{0,61},{1,62},{2,63},{3,0},{4,1},{5,2},{6,3},{7,4},{8,5},{9,6},{10... | collective-permute-start | bytes 786440 | tf_op jit(solution)/shard_map/ppermute | solution.py:15
where the time goes:
time: 292 us; the launch traced here: 291 us
  blocking collectives  191 us (65%)
  starting transfers between devices  51.7 us (18%)
  matrix products  23 us (8%)
  waiting for transfers between devices  10.6 us (4%)
  local copies, waits for them, and re-layouts  8.31 us (3%)
  other arithmetic  5.18 us (2%)
    psum x1, blocking collectives, body(): summed = lax.psum(terms, ('dp', 'ctx'))  191 us
    ppermute x14, starting transfers between devices, from_behind(): return lax.ppermute(value, axis, pairs)  51.7 us
    ppermute x14, waiting for transfers between devices, from_behind(): return lax.ppermute(value, axis, pairs)  10.6 us
  transfers between devices with their start and end apart: 14, of which 3 were waited for; matrix products, arithmetic and copies ran while one was open for 10% of the time, Pallas kernels for 0%

commit v1 on v0

--- a/solution.py
+++ b/solution.py
@@ -102,7 +102,9 @@
     width_rows = local.shape[1]
     share = width_rows // cycle_size
     terms = jnp.einsum("rd,rf->df", local, joined, preferred_element_type=jnp.float32)
-    summed = lax.psum(terms, ("dp", "ctx"))
+    summed = terms
+    for it in ("ctx", "dp"):
+        summed = jax.lax.psum(summed, it)
     mine = lax.dynamic_slice_in_dim(summed, myself * share, share, 0)
     grad_wq = mine[:, :features].astype(jnp.bfloat16)
     grad_wk = mine[:, features:].astype(jnp.bfloat16)

time: 292 us -> 807 us (2.76); the launches traced: 291 us -> 794 us
  waiting for transfers between devices: 10.6 us -> 510 us
  blocking collectives: 191 us -> 159 us
  starting transfers between devices: 51.7 us -> 78 us
  between operations: 1.85 us -> 15.3 us
    psum x0 -> x1, waiting for transfers between devices: none -> 490 us  [body(): summed = jax.lax.psum(summed, it)]
    psum x1, blocking collectives: 191 us -> 159 us  [body(): summed = jax.lax.psum(summed, it)]
    ppermute x14, starting transfers between devices: 51.7 us -> 78 us  [from_behind(): return lax.ppermute(value, axis, pairs)]
    ppermute x14, waiting for transfers between devices: 10.6 us -> 19.4 us  [from_behind(): return lax.ppermute(value, axis, pairs)]
  transfers between devices with their start and end apart: 14 -> 15, of which waited for: 3 -> 9; matrix products, arithmetic and copies ran while one was open for 10% -> 3% of each run, Pallas kernels for 0% -> 0%
where the time goes in v1:
time: 807 us; the launch traced here: 794 us
  waiting for transfers between devices  510 us (63%)
  blocking collectives  159 us (20%)
  starting transfers between devices  78 us (10%)
  matrix products  21.6 us (3%)
  between operations  15.3 us (2%)
    psum x1, waiting for transfers between devices, body(): summed = jax.lax.psum(summed, it)  490 us
    psum x1, blocking collectives, body(): summed = jax.lax.psum(summed, it)  159 us
    ppermute x14, starting transfers between devices, from_behind(): return lax.ppermute(value, axis, pairs)  78 us
    ppermute x14, waiting for transfers between devices, from_behind(): return lax.ppermute(value, axis, pairs)  19.4 us
  transfers between devices with their start and end apart: 15, of which 9 were waited for; matrix products, arithmetic and copies ran while one was open for 3% of the time, Pallas kernels for 0%

profile of v1, /device:TPU:7, one launch (start us, length us, event | category | flops | bytes accessed | tf_op | source)
XLA Modules:
  0.0 793.6 jit_solution(7418911149814118253)
XLA Ops:
  7.2 1.2 copy.87
  8.4 4.9 collective-permute-start.1
  13.4 1.5 fusion.20
  14.9 0.7 copy.157
  15.6 1.9 collective-permute-start
  18.3 1.0 select_reduce_fusion
  19.4 0.7 copy.86
  20.3 1.0 reshape_squeeze.7
  21.3 1.8 convolution_convert_fusion.3
  23.7 1.4 multiply_convert_fusion.3
  25.9 4.1 collective-permute-start.10
  30.4 1.5 multiply_convert_fusion.2
  31.9 0.5 fusion.14
  32.4 0.9 collective-permute-done.10
  33.6 6.8 collective-permute-start.11
  40.4 1.9 collective-permute-start.3
  42.3 3.9 collective-permute-start.2
  46.2 1.3 convolution_add_fusion.2
  47.5 2.3 collective-permute-done.2
  49.8 0.5 multiply_convert_fusion.1
  50.4 0.5 fusion.13
  51.2 6.7 collective-permute-start.12
  57.9 1.9 collective-permute-start.5
  59.9 4.1 collective-permute-start.4
  64.3 3.0 collective-permute-done.4
  67.3 0.5 multiply_convert_fusion
  67.9 0.5 fusion.12
  68.7 11.1 %collective-permute-start.13 = (bf16[256,4,128]{0,2,1:T(8,128)(2,1)S(1)}, bf16[256,4,128]{0,2,1:T(8,128)(2,1)S(1)}, u32[]{:S(2)}, u32[]{:S(2)}) collective-permute-start(bf16[256,4,128]{0,2,1:T(8,128)(2,1)S(1)} %add_convert_fusion), channel_id=1, source_target_pairs={{0,61},{1,62},{2,63},{3,0},{4,1},{5,2},{6,3},{7,4},{8,5},{9,6},{10... | collective-permute-start | bytes 786440 | tf_op jit(solution)/shard_map/ppermute | solution.py:15
  80.2 3.0 collective-permute-done.13
  83.2 2.7 convolution_bitcast_fusion
  85.9 2.1 fusion.18
  88.0 1.9 collective-permute-start.6
  90.0 1.4 fusion.44
  91.4 2.2 collective-permute-done.6
  93.6 1.3 add_convert_fusion.5
  94.9 6.9 collective-permute-start.7
  102.5 2.6 collective-permute-done.7
  105.2 6.8 collective-permute-start.8
  112.6 2.9 collective-permute-done.8
  115.6 0.8 add_convert_fusion.3
  116.3 14.9 %collective-permute-start.9 = (bf16[256,4,128]{2,0,1:T(8,128)(2,1)}, bf16[256,4,128]{2,0,1:T(8,128)(2,1)S(1)}, u32[]{:S(2)}, u32[]{:S(2)}) collective-permute-start(bf16[256,4,128]{2,0,1:T(8,128)(2,1)} %add_convert_fusion.3), channel_id=1, source_target_pairs={{0,61},{1,62},{2,63},{3,0},{4,1},{5,2},{6,3},{7,4},{8,5},{9,6},{10... | collective-permute-start | bytes 786440 | tf_op jit(solution)/shard_map/ppermute | solution.py:15
  131.5 0.8 copy.117
  132.4 2.4 collective-permute-done.9
  135.0 0.8 copy.118
  135.8 490.4 %all-reduce.3.cloned.1.call-done = f32[1024,1024]{0,1:T(8,128)} async-done(((f32[1024,1024]{0,1:T(8,128)}), f32[1024,1024]{0,1:T(8,128)}) %all-reduce.3.cloned.1.call-update) | async-done | bytes 4194320 | tf_op jit(solution)/shard_map/psum | solution.py:107
  626.3 158.9 %all-reduce.4 = bf16[1024,1024]{0,1:T(8,128)(2,1)S(1)} all-reduce(f32[1024,1024]{0,1:T(8,128)} %all-reduce.3.cloned.1.call-done), channel_id=1, replica_groups=mesh['dp'=8,'ctx'=64] {'dp'}, use_global_device_ids=true, to_apply=%region_10.11 | all-reduce | flops 1048576 | bytes 6291456 | tf_op jit(solution)/shard_map/psum | solution.py:107
  785.3 0.7 copy.120
  786.0 0.7 copy.119
  (60 shorter events, 5.4 us)
Async XLA Ops:
  7.2 6.2 copy-start
  7.2 619.1 %all-reduce.3.cloned.1.call-start = ((), (), s32[]{:S(2)}) async-start(), calls=%async_computation | async-start | bytes 8388608 | tf_op jit(solution)/shard_map/psum | solution.py:107
  8.4 16.7 %copy-start.2 = (bf16[1,256,512]{1,2,0:T(8,128)(2,1)}, bf16[1,256,512]{1,2,0:T(8,128)(2,1)S(1)}, u32[]{:S(2)}) copy-start(bf16[1,256,512]{1,2,0:T(8,128)(2,1)S(1)} %copy.87) | copy-start | bytes 786436
  8.4 23.5 %collective-permute-start.1 = (bf16[256,4,128]{0,2,1:T(8,128)(2,1)S(1)}, bf16[256,4,128]{0,2,1:T(8,128)(2,1)S(1)}, u32[]{:S(2)}, u32[]{:S(2)}) collective-permute-start(bf16[256,4,128]{0,2,1:T(8,128)(2,1)S(1)} %bitcast.101), channel_id=1, source_target_pairs={{0,1},{1,2},{2,3},{3,4},{4,5},{5,6},{6,7},{7,8},{8,9},{9,10},{10,1... | collective-permute-start | bytes 786440 | tf_op jit(solution)/shard_map/ppermute | solution.py:15
  15.6 14.8 %collective-permute-start = (bf16[256,4,128]{2,0,1:T(8,128)(2,1)}, bf16[256,4,128]{2,0,1:T(8,128)(2,1)}, u32[]{:S(2)}, u32[]{:S(2)}) collective-permute-start(bf16[256,4,128]{2,0,1:T(8,128)(2,1)} %bitcast.88), channel_id=1, source_target_pairs={{0,1},{1,2},{2,3},{3,4},{4,5},{5,6},{6,7},{7,8},{8,9},{9,10},{10,1... | collective-permute-start | bytes 786440 | tf_op jit(solution)/shard_map/ppermute | solution.py:15
  25.9 7.4 collective-permute-start.10
  31.9 15.6 %copy-start.4 = (bf16[256,4,128]{0,2,1:T(8,128)(2,1)}, bf16[256,4,128]{0,2,1:T(8,128)(2,1)S(1)}, u32[]{:S(2)}) copy-start(bf16[256,4,128]{0,2,1:T(8,128)(2,1)S(1)} %collective-permute-done.1) | copy-start | bytes 786436
  33.6 17.6 %collective-permute-start.11 = (bf16[256,4,128]{0,2,1:T(8,128)(2,1)S(1)}, bf16[256,4,128]{0,2,1:T(8,128)(2,1)S(1)}, u32[]{:S(2)}, u32[]{:S(2)}) collective-permute-start(bf16[256,4,128]{0,2,1:T(8,128)(2,1)S(1)} %add_convert_fusion.2), channel_id=1, source_target_pairs={{0,1},{1,2},{2,3},{3,4},{4,5},{5,6},{6,7},{7,8},{8,9},{9,10},{10,1... | collective-permute-start | bytes 786440 | tf_op jit(solution)/shard_map/ppermute | solution.py:15
  40.4 10.0 %collective-permute-start.3 = (bf16[256,4,128]{0,2,1:T(8,128)(2,1)S(1)}, bf16[256,4,128]{0,2,1:T(8,128)(2,1)S(1)}, u32[]{:S(2)}, u32[]{:S(2)}) collective-permute-start(bf16[256,4,128]{0,2,1:T(8,128)(2,1)S(1)} %collective-permute-done.1), channel_id=1, source_target_pairs={{0,1},{1,2},{2,3},{3,4},{4,5},{5,6},{6,7},{7,8},{8,9},{9,10},{10,1... | collective-permute-start | bytes 786440 | tf_op jit(solution)/shard_map/ppermute | solution.py:15
  42.3 7.5 collective-permute-start.2
  50.4 7.6 copy-start.6
  51.2 17.4 %collective-permute-start.12 = (bf16[256,4,128]{0,2,1:T(8,128)(2,1)S(1)}, bf16[256,4,128]{0,2,1:T(8,128)(2,1)S(1)}, u32[]{:S(2)}, u32[]{:S(2)}) collective-permute-start(bf16[256,4,128]{0,2,1:T(8,128)(2,1)S(1)} %add_convert_fusion.1), channel_id=1, source_target_pairs={{0,1},{1,2},{2,3},{3,4},{4,5},{5,6},{6,7},{7,8},{8,9},{9,10},{10,1... | collective-permute-start | bytes 786440 | tf_op jit(solution)/shard_map/ppermute | solution.py:15
  57.9 9.9 %collective-permute-start.5 = (bf16[256,4,128]{0,2,1:T(8,128)(2,1)S(1)}, bf16[256,4,128]{0,2,1:T(8,128)(2,1)S(1)}, u32[]{:S(2)}, u32[]{:S(2)}) collective-permute-start(bf16[256,4,128]{0,2,1:T(8,128)(2,1)S(1)} %collective-permute-done.3), channel_id=1, source_target_pairs={{0,1},{1,2},{2,3},{3,4},{4,5},{5,6},{6,7},{7,8},{8,9},{9,10},{10,1... | collective-permute-start | bytes 786440 | tf_op jit(solution)/shard_map/ppermute | solution.py:15
  59.9 7.4 collective-permute-start.4
  67.9 0.8 copy-start.8
  67.9 15.3 %copy-start.1 = (bf16[1,256,1024]{2,1,0:T(8,128)(2,1)S(1)}, bf16[1,256,1024]{2,1,0:T(8,128)(2,1)}, u32[]{:S(2)}) copy-start(bf16[1,256,1024]{2,1,0:T(8,128)(2,1)} %param.8) | copy-start | bytes 1572868
  68.7 14.4 %collective-permute-start.13 = (bf16[256,4,128]{0,2,1:T(8,128)(2,1)S(1)}, bf16[256,4,128]{0,2,1:T(8,128)(2,1)S(1)}, u32[]{:S(2)}, u32[]{:S(2)}) collective-permute-start(bf16[256,4,128]{0,2,1:T(8,128)(2,1)S(1)} %add_convert_fusion), channel_id=1, source_target_pairs={{0,61},{1,62},{2,63},{3,0},{4,1},{5,2},{6,3},{7,4},{8,5},{9,6},{10... | collective-permute-start | bytes 786440 | tf_op jit(solution)/shard_map/ppermute | solution.py:15
  85.9 4.1 copy-start.3
  85.9 15.9 %copy-start.5 = (bf16[256,4,128]{0,2,1:T(8,128)(2,1)S(1)}, bf16[256,4,128]{0,2,1:T(8,128)(2,1)}, u32[]{:S(2)}) copy-start(bf16[256,4,128]{0,2,1:T(8,128)(2,1)} %copy-done.4) | copy-start | bytes 786436
  88.0 5.5 collective-permute-start.6
  90.0 22.0 %copy-start.7 = (bf16[256,4,128]{0,2,1:T(8,128)(2,1)S(1)}, bf16[256,4,128]{0,2,1:T(8,128)(2,1)}, u32[]{:S(2)}) copy-start(bf16[256,4,128]{0,2,1:T(8,128)(2,1)} %copy-done.6) | copy-start | bytes 786436
  94.9 36.3 %copy-start.9 = (bf16[256,4,128]{0,2,1:T(8,128)(2,1)S(1)}, bf16[256,4,128]{0,2,1:T(8,128)(2,1)}, u32[]{:S(2)}) copy-start(bf16[256,4,128]{0,2,1:T(8,128)(2,1)} %copy-done.8) | copy-start | bytes 786436
  94.9 10.2 %collective-permute-start.7 = (bf16[256,4,128]{2,0,1:T(8,128)(2,1)S(1)}, bf16[256,4,128]{2,0,1:T(8,128)(2,1)S(1)}, u32[]{:S(2)}, u32[]{:S(2)}) collective-permute-start(bf16[256,4,128]{2,0,1:T(8,128)(2,1)S(1)} %add_convert_fusion.5), channel_id=1, source_target_pairs={{0,1},{1,2},{2,3},{3,4},{4,5},{5,6},{6,7},{7,8},{8,9},{9,10},{10,1... | collective-permute-start | bytes 786440 | tf_op jit(solution)/shard_map/ppermute | solution.py:15
  105.2 10.4 %collective-permute-start.8 = (bf16[256,4,128]{2,0,1:T(8,128)(2,1)S(1)}, bf16[256,4,128]{2,0,1:T(8,128)(2,1)S(1)}, u32[]{:S(2)}, u32[]{:S(2)}) collective-permute-start(bf16[256,4,128]{2,0,1:T(8,128)(2,1)S(1)} %add_convert_fusion.4), channel_id=1, source_target_pairs={{0,1},{1,2},{2,3},{3,4},{4,5},{5,6},{6,7},{7,8},{8,9},{9,10},{10,1... | collective-permute-start | bytes 786440 | tf_op jit(solution)/shard_map/ppermute | solution.py:15
  116.3 18.5 %collective-permute-start.9 = (bf16[256,4,128]{2,0,1:T(8,128)(2,1)}, bf16[256,4,128]{2,0,1:T(8,128)(2,1)S(1)}, u32[]{:S(2)}, u32[]{:S(2)}) collective-permute-start(bf16[256,4,128]{2,0,1:T(8,128)(2,1)} %add_convert_fusion.3), channel_id=1, source_target_pairs={{0,61},{1,62},{2,63},{3,0},{4,1},{5,2},{6,3},{7,4},{8,5},{9,6},{10... | collective-permute-start | bytes 786440 | tf_op jit(solution)/shard_map/ppermute | solution.py:15
Sparse Core Ops, SparseCore 0:
  86.0 540.1 all-reduce.2
